TPU v7x, 32 devices: a whole 2x2x4 slice. The times are simulated.
32 devices in a mesh: row: 8 (over y, x, core), col: 4 (over z).
Axes of the slice: x: 2, y: 2, z: 4, core: 2. Of those that a mesh axis runs over, the one named last changes fastest.
Arguments:
- hidden_in: bfloat16 [1152, 2048], P('col', 'row'), may hold values from -21 to 21
- state: float32 [128, 2048, 1152], P('col', 'row'), may hold values from -4 to 4
- attn_norm_gain: bfloat16 [2048], replicated, may hold values from 0.099609375 to 1.8984375
- w_query: bfloat16 [2048, 2048], P(None, 'row'), may hold values from -0.125 to 0.125
- w_key: bfloat16 [2048, 2048], P(None, 'row'), may hold values from -0.125 to 0.125
- w_value: bfloat16 [2048, 2048], P(None, 'row'), may hold values from -0.125 to 0.125
- w_gate: bfloat16 [2048, 2048], P(None, 'row'), may hold values from -0.125 to 0.125
- w_decay: bfloat16 [2048, 16], replicated, may hold values from -0.125 to 0.125
- w_beta: bfloat16 [2048, 16], replicated, may hold values from -0.125 to 0.125
- decay_log: float32 [16], replicated, may hold values from -3 to 1.5
- decay_bias: float32 [16], replicated, may hold values from -2 to 1
- head_gain: float32 [128], replicated, may hold values from 0.1 to 1.9
- w_out: bfloat16 [2048, 2048], P('row'), may hold values from -0.125 to 0.125
- final_gain: bfloat16 [2048], P('row'), may hold values from 0.099609375 to 1.8984375
- lm_weight: bfloat16 [2048, 20480], P(None, ('row', 'col')), may hold values from -0.28726213 to 0.28726213
- token_ids: int32 [1152], replicated, may hold values from 0 to 20479
- ref_logprob: float32 [1152], replicated, may hold values from -16 to -6
Outputs:
- new_state: float32 [128, 2048, 1152], P('col', 'row')
- logprob: float32 [1152], replicated
- entropy: float32 [1152], replicated
- kl: float32 [1152], replicated
All inputs are finite; a program needn't handle non-finite values.
Results may differ from a plain program's by a relative error of at most 0.0014.
The roundings to bfloat16 on the way count: a program that leaves them out, or rounds other values in their place, can miss the bound.
Values may be sent and summed in bfloat16 or wider, within the bound.
A program may use at most 128 MiB of HBM per device.

v0:
```python
import jax
import jax.numpy as jnp
from jax import lax
from jax.sharding import PartitionSpec as P

D = 2048
HEADS = 16
DK = 128
DV = 128


def partner_2(block, axis, apart):
    count = lax.axis_size(axis)
    route = []
    for low in range(count):
        high = low | 1 << apart
        if high != low and high < count:
            route += [(low, high), (high, low)]
    return lax.ppermute(block, axis, route)


def project(weight, normed):
    return lax.dot_general(
        weight, normed, (((0,), (1,)), ((), ())), preferred_element_type=jnp.float32
    )


def per_device(
    hidden_in,
    state,
    attn_norm_gain,
    w_query,
    w_key,
    w_value,
    w_gate,
    w_decay,
    w_beta,
    decay_log,
    decay_bias,
    head_gain,
    w_out,
    final_gain,
    lm_weight,
    token_ids,
    ref_logprob,
):
    highest = lax.Precision.HIGHEST
    row_count = lax.axis_size("row")
    col_count = lax.axis_size("col")
    row_index = lax.axis_index("row")
    col_index = lax.axis_index("col")
    group = max(1, row_count // HEADS)
    local_heads = max(1, HEADS // row_count)
    first_head = row_index // group * local_heads
    value_cols = w_value.shape[1]
    value_part = value_cols // local_heads
    block_rows = hidden_in.shape[0]
    key_rows = state.shape[0]
    batch = state.shape[2]
    vocab_dev = lm_weight.shape[1]
    whole_rows = lax.all_gather(hidden_in, "row", axis=1, tiled=True)
    xfull = whole_rows.astype(jnp.float32)
    normed = (
        xfull
        * lax.rsqrt(jnp.mean(xfull * xfull, axis=1, keepdims=True) + 1e-06)
        * attn_norm_gain.astype(jnp.float32)
    ).astype(jnp.bfloat16)
    raw_pair = jnp.stack([project(w_query, normed), project(w_key, normed)]).astype(jnp.bfloat16)
    raw_pair = lax.optimization_barrier(raw_pair)
    for level in range(group.bit_length() - 1):
        partner = partner_2(raw_pair, "row", level)
        upper = row_index >> level & 1 == 1
        raw_pair = jnp.where(
            upper,
            jnp.concatenate([partner, raw_pair], axis=1),
            jnp.concatenate([raw_pair, partner], axis=1),
        )
    pair_f = raw_pair.astype(jnp.float32).reshape(2, local_heads, DK, block_rows)
    unit_pair = (
        pair_f * lax.rsqrt(jnp.sum(pair_f * pair_f, axis=2, keepdims=True) + 1e-06)
    ).astype(jnp.bfloat16)
    tiles_qk = lax.all_to_all(unit_pair, "col", split_axis=2, concat_axis=3, tiled=True)
    query = tiles_qk[0].astype(jnp.float32)
    key = tiles_qk[1].astype(jnp.float32)
    value_t = project(w_value, normed)
    gate_t = project(w_gate, normed)
    decay_in = lax.dynamic_slice_in_dim(project(w_decay, normed), first_head, local_heads, 0)
    beta_in = lax.dynamic_slice_in_dim(project(w_beta, normed), first_head, local_heads, 0)
    rate = jnp.exp(lax.dynamic_slice_in_dim(decay_log, first_head, local_heads, 0))
    bias = lax.dynamic_slice_in_dim(decay_bias, first_head, local_heads, 0)
    alpha_t = jnp.exp(-rate[:, None] * jax.nn.softplus(decay_in + bias[:, None]))
    beta_t = jax.nn.sigmoid(beta_in)
    value_all, gate_all, alpha, beta = (
        lax.all_gather(value_t, "col", axis=1, tiled=True),
        lax.all_gather(gate_t, "col", axis=1, tiled=True),
        lax.all_gather(alpha_t, "col", axis=1, tiled=True),
        lax.all_gather(beta_t, "col", axis=1, tiled=True),
    )
    tiles = state.reshape(key_rows, local_heads, value_part, batch)
    value4 = value_all.reshape(local_heads, value_part, batch)
    key_major = jnp.transpose(key, (1, 0, 2))
    recall, answer, intersection = lax.psum(
        (
            jnp.einsum("khvb,hkb->hvb", tiles, key, precision=highest),
            jnp.einsum("khvb,hkb->hvb", tiles, query, precision=highest),
            jnp.sum(key * query, axis=1),
        ),
        "col",
    )
    write = beta[:, None, :] * (value4 - alpha[:, None, :] * recall)
    updated = alpha[None, :, None, :] * tiles + key_major[:, :, None, :] * write[None]
    readout = alpha[:, None, :] * answer + intersection[:, None, :] * write
    power = jnp.sum(readout * readout, axis=1)
    for level in range(group.bit_length() - 1):
        power = power + partner_2(power, "row", level)
    gain_part = lax.dynamic_slice_in_dim(head_gain, row_index % group * value_part, value_part, 0)
    gate4 = gate_all.reshape(local_heads, value_part, batch)
    mixed = (
        readout
        * lax.rsqrt(power / DV + 1e-05)[:, None, :]
        * gain_part[None, :, None]
        * jax.nn.silu(gate4)
    )
    mixed_heads = mixed.reshape(value_cols, batch).astype(jnp.bfloat16)
    mine = lax.dynamic_slice_in_dim(mixed_heads, col_index * block_rows, block_rows, 1)
    branch = lax.psum_scatter(
        lax.dot_general(w_out, mine, (((0,), (0,)), ((), ())), preferred_element_type=jnp.float32),
        "row",
        scatter_dimension=0,
        tiled=True,
    )
    hidden = hidden_in.astype(jnp.float32) + branch.T
    energy = lax.psum(jnp.sum(hidden * hidden, axis=1), "row")
    final = (
        hidden * lax.rsqrt(energy / D + 1e-06)[:, None] * final_gain.astype(jnp.float32)[None, :]
    ).astype(jnp.bfloat16)
    tall = lax.all_gather(final, "col", axis=0, tiled=True)
    logits = jnp.dot(
        lax.all_gather(tall, "row", axis=1, tiled=True),
        lm_weight,
        preferred_element_type=jnp.float32,
    )
    vocab_start = (row_index * col_count + col_index) * vocab_dev
    hits = jnp.arange(vocab_dev, dtype=jnp.int32)[None, :] + vocab_start == token_ids[:, None]
    local_pick = jnp.sum(jnp.where(hits, logits, jnp.zeros_like(logits)), axis=1)
    local_top = jnp.max(logits, axis=1)
    expo = jnp.exp(logits - local_top[:, None])
    local_total = jnp.sum(expo, axis=1)
    local_weighted = jnp.sum(expo * logits, axis=1)
    top = lax.pmax(local_top, ("row", "col"))
    shrink = jnp.exp(local_top - top)
    total, weighted, picked = lax.psum(
        (local_total * shrink, local_weighted * shrink, local_pick), ("row", "col")
    )
    lse = top + jnp.log(total)
    logprob = picked - lse
    entropy = lse - weighted / total
    gap = jnp.clip(ref_logprob - logprob, -20.0, 20.0)
    kl = jnp.minimum(jnp.exp(gap) - gap - 1.0, 10.0)
    new_state = updated.reshape(key_rows, value_cols, batch)
    return (new_state, logprob, entropy, kl)


def solution(mesh):
    in_specs = (
        P("col", "row"),
        P("col", "row", None),
        P(),
        P(None, "row"),
        P(None, "row"),
        P(None, "row"),
        P(None, "row"),
        P(),
        P(),
        P(),
        P(),
        P(),
        P("row", None),
        P("row"),
        P(None, ("row", "col")),
        P(),
        P(),
    )
    out_specs = (P("col", "row", None), P(), P(), P())
    return jax.shard_map(
        per_device, mesh=mesh, in_specs=in_specs, out_specs=out_specs, check_vma=False
    )
```

profile of v0, /device:TPU:0, one launch (start us, length us, event | category | flops | bytes accessed | tf_op | source)
XLA Modules:
  0.0 437.5 jit_solution(9611972325087262936)
XLA Ops:
  7.2 0.7 all-gather.7.cloned.1.call-update
  8.0 0.7 convert_element_type.38
  8.7 28.0 %all-gather.7.cloned.1.call-done = bf16[288,2048]{1,0:T(8,128)(2,1)} async-done(((bf16[288,256]{1,0:T(8,128)(2,1)}), bf16[288,2048]{1,0:T(8,128)(2,1)}) %all-gather.7.cloned.1.call-update) | async-done | bytes 1179664 | tf_op jit(solution)/shard_map/all_gather | solution.py:61
  36.7 1.7 fusion.2
  38.7 1.0 copy-done.2
  39.8 1.2 convolution_bitcast_fusion.2
  41.0 2.2 fusion.8
  44.1 1.4 multiply_reduce_fusion.4
  45.5 1.1 copy.79
  46.9 1.1 copy.81
  47.9 4.6 %all-to-all-start = ((bf16[2,2,128,288]{3,1,0,2:T(2,128)(2,1)}), bf16[2,2,128,288]{3,1,0,2:T(2,128)(2,1)S(1)}, u32[]{:S(2)}, u32[]{:S(2)}) async-start(bf16[2,2,128,288]{3,1,0,2:T(2,128)(2,1)} %copy.81), calls=%async_computation | async-start | bytes 786432 | tf_op jit(solution)/shard_map/all_to_all | solution.py:82
  52.5 2.8 convolution_bitcast_fusion.1
  55.4 20.5 %all-to-all-done = bf16[2,2,128,288]{3,1,0,2:T(2,128)(2,1)S(1)} async-done(((bf16[2,2,128,288]{3,1,0,2:T(2,128)(2,1)}), bf16[2,2,128,288]{3,1,0,2:T(2,128)(2,1)S(1)}, u32[]{:S(2)}, u32[]{:S(2)}) %all-to-all-start) | async-done | bytes 294944 | tf_op jit(solution)/shard_map/all_to_all | solution.py:82
  76.0 0.7 copy-done.9
  77.9 17.6 %multiply_reduce_fusion = (f32[2,1152,128]{1,2,0:T(8,128)}, f32[2,1152,128]{1,2,0:T(8,128)}) fusion(f32[2,1152,32,128]{1,3,0,2:T(8,128)} %bitcast.104, f32[2,1152,32]{1,0,2:T(2,128)S(1)} %copy.112, f32[2,1152,32]{1,0,2:T(2,128)S(1)} %copy.111), kind=kLoop, calls=%fused_computation.2 | loop fusion | flops 37158912 | bytes 40697856
  95.5 3.3 copy.107
  98.8 3.4 copy.99
  103.1 1.7 fusion.28
  104.8 13.3 %all-gather.1 = f32[4,288,2]{1,2,0:T(2,128)S(1)} all-gather(f32[1,288,2]{1,2,0:T(2,128)S(1)} %divide_bitcast_fusion), channel_id=1, replica_groups=mesh['row'=8,'col'=4] {'col'}, dimensions={0}, use_global_device_ids=true | all-gather | bytes 11520 | tf_op jit(solution)/shard_map/all_gather | solution.py:97
  118.2 1.7 fusion.27
  120.1 13.7 %all-gather = f32[4,288,2]{1,2,0:T(2,128)S(1)} all-gather(f32[1,288,2]{1,2,0:T(2,128)S(1)} %fusion.18), channel_id=1, replica_groups=mesh['row'=8,'col'=4] {'col'}, dimensions={0}, use_global_device_ids=true | all-gather | bytes 11520 | tf_op jit(solution)/shard_map/all_gather | solution.py:96
  133.9 1.1 copy.86
  135.2 1.1 multiply_reduce_fusion.5
  136.4 11.1 %psum.51 = f32[2,1152]{1,0:T(2,128)S(1)} all-reduce(f32[2,1152]{1,0:T(2,128)S(1)} %reduce_sum.77), channel_id=1, replica_groups=mesh['row'=8,'col'=4] {'col'}, use_global_device_ids=true, to_apply=%region_5.6 | all-reduce | flops 2304 | bytes 18432 | tf_op jit(solution)/shard_map/psum | solution.py:102
  147.5 1.1 copy.89
  148.6 2.8 reshape.76
  151.4 2.8 reshape.78
  154.2 54.1 %all-reduce.4.cloned.1.call-done = (f32[2,128,1152]{1,0,2:T(2,128)}, f32[2,128,1152]{1,0,2:T(2,128)}) async-done(((f32[2,128,1152]{1,0,2:T(2,128)}, f32[2,128,1152]{1,0,2:T(2,128)}), (f32[2,128,1152]{1,0,2:T(2,128)}, f32[2,128,1152]{1,0,2:T(2,128)})) %all-reduce.4.cloned.1.call-update) | async-done | bytes 2359312 | tf_op jit(solution)/shard_map/psum | solution.py:102
  208.2 7.9 %multiply_reduce_fusion.3 = (f32[2,1152]{0,1:T(8,128)S(1)}, f32[2,128,1152]{1,0,2:T(2,128)S(1)}) fusion(f32[2,1152]{0,1:T(8,128)} %copy.89, f32[2,128,1152]{1,0,2:T(2,128)} %get-tuple-element.13, f32[2,1152]{0,1:T(8,128)S(1)} %copy.77, f32[2,128,1152]{1,0,2:T(2,128)} %reshape.76, f32[2,128,1152]{1,0,2:T(2,128)} %get-tuple-element.12, f32[2,1152]{0,1:T(8,128)} %copy.86), kind=kLoop, calls=%fused_computation.16 | loop fusion | flops 2356992 | bytes 4755456 | tf_op jit(solution)/shard_map/reduce_sum | solution.py:113
  216.2 1.4 copy-done.4
  217.6 4.6 %fusion.6 = bf16[2,128,1152]{1,0,2:T(2,128)(2,1)S(1)} fusion(f32[2,128,1152]{1,0,2:T(2,128)S(1)} %copy-done.7, f32[128]{0:T(128)S(1)} %copy-done.16, f32[2,1152]{0,1:T(8,128)S(1)} %add_rsqrt_fusion, f32[2,128,1152]{1,0,2:T(2,128)S(1)} %get-tuple-element.17, f32[2,1152]{0,1:T(8,128)S(1)} %copy-done.4, f32[2,128,1152]{1,0,2:T(2,128)S(1)} %copy-done.5, ...), kind=kLoop, calls=%fused_computation.19 | loop fusion | flops 3244032 | bytes 4156928 | tf_op jit(solution)/shard_map/convert_element_type | solution.py:124
  222.3 1.1 copy-done.11
  223.5 1.9 convolution_bitcast_fusion
  225.4 0.6 copy-done.21
  226.0 40.9 %reduce-scatter.2.cloned.1.call-done = f32[256,288]{0,1:T(8,128)} async-done(((f32[2048,288]{0,1:T(8,128)}), f32[256,288]{0,1:T(8,128)}) %reduce-scatter.2.cloned.1.call-update) | async-done | bytes 294928 | tf_op jit(solution)/shard_map/reduce_scatter | solution.py:126
  266.9 1.1 multiply_reduce_fusion.6
  268.0 12.5 %psum.52 = f32[288]{0:T(512)S(1)} all-reduce(f32[288]{0:T(512)S(1)} %multiply_reduce_fusion.6), channel_id=1, replica_groups=mesh['row'=8,'col'=4] {'row'}, use_global_device_ids=true, to_apply=%region_9.10 | all-reduce | flops 288 | bytes 2304 | tf_op jit(solution)/shard_map/psum | solution.py:133
  280.5 1.1 multiply_convert_fusion
  281.6 16.7 %all_gather.26 = bf16[1152,256]{1,0:T(8,128)(2,1)} all-gather(bf16[288,256]{1,0:T(8,128)(2,1)S(1)} %multiply_convert_fusion), channel_id=1, replica_groups=mesh['row'=8,'col'=4] {'col'}, dimensions={0}, use_global_device_ids=true | all-gather | bytes 737280 | tf_op jit(solution)/shard_map/all_gather | solution.py:137
  298.6 3.4 copy.109
  302.0 1.2 copy-done.8
  303.2 28.9 %fusion = f32[32,256,1152]{2,1,0:T(8,128)} fusion(f32[32,256,1152]{2,1,0:T(8,128)} %param.18, f32[256,1152]{1,0:T(8,128)S(1)} %bitcast.107, f32[32,2,1152]{2,1,0:T(2,128)S(1)} %copy.84, f32[256,1152]{1,0:T(8,128)S(1)} %bitcast.108), kind=kLoop, calls=%fused_computation.1 | loop fusion | flops 28311552 | bytes 78151680 | tf_op jit(solution)/shard_map/add | solution.py:111
  332.1 6.9 %all-gather.13.cloned.1.call-done = bf16[1152,2048]{1,0:T(8,128)(2,1)} async-done(((bf16[1152,256]{1,0:T(8,128)(2,1)}), bf16[1152,2048]{1,0:T(8,128)(2,1)}) %all-gather.13.cloned.1.call-update) | async-done | bytes 4718608 | tf_op jit(solution)/shard_map/all_gather | solution.py:139
  339.0 7.6 %fusion.26 = (f32[1152]{0:T(1024)S(1)}, f32[1152,640]{0,1:T(8,128)}) fusion(bf16[1152,2048]{1,0:T(8,128)(2,1)} %all-gather.13.cloned.1.call-done, bf16[2048,640]{1,0:T(8,128)(2,1)S(1)} %copy-done), kind=kOutput, calls=%fused_computation.68 | convolution fusion | flops 3020635136 | bytes 10293760 | tf_op jit(solution)/shard_map/dot_general | solution.py:138
  346.6 39.3 %pmax.7 = f32[1152]{0:T(1024)S(1)} all-reduce(f32[1152]{0:T(1024)S(1)} %get-tuple-element.25), channel_id=1, replica_groups=mesh['row'=8,'col'=4] {'row','col'}, use_global_device_ids=true, to_apply=%region_13.14 | all-reduce | flops 1152 | bytes 9216 | tf_op jit(solution)/shard_map/pmax | solution.py:150
  385.9 2.7 multiply_reduce_fusion.2
  388.7 41.3 %all-reduce = (f32[1152]{0:T(1024)S(1)}, f32[1152]{0:T(1024)S(1)}, f32[1152]{0:T(1024)S(1)}) all-reduce(f32[1152]{0:T(1024)S(1)} %get-tuple-element.8, f32[1152]{0:T(1024)S(1)} %get-tuple-element.24, f32[1152]{0:T(1024)S(1)} %get-tuple-element.23), channel_id=1, replica_groups=mesh['row'=8,'col'=4] {'row','col'}, use_global_device_ids=true, to_apply=%region_11.12 | all-reduce | flops 3456 | bytes 27648 | tf_op jit(solution)/shard_map/psum | solution.py:152
  430.0 0.6 fusion.12
  (86 shorter events, 4.9 us)
Async XLA Ops:
  7.2 331.9 %copy-start = (bf16[2048,640]{1,0:T(8,128)(2,1)S(1)}, bf16[2048,640]{1,0:T(8,128)(2,1)}, u32[]{:S(2)}) copy-start(bf16[2048,640]{1,0:T(8,128)(2,1)} %param.31) | copy-start | bytes 7864324
  7.2 29.5 %all-gather.7.cloned.1.call-start = ((), (), s32[]{:S(2)}) async-start(), calls=%async_computation.2 | async-start | bytes 1327104 | tf_op jit(solution)/shard_map/all_gather | solution.py:61
  7.9 140.7 %all-gather.9.cloned.1.call-start = ((), (), s32[]{:S(2)}) async-start(), calls=%async_computation.3 | async-start | bytes 1474560 | tf_op jit(solution)/shard_map/all_gather | solution.py:94
  36.7 1.7 copy-start.6
  38.4 1.4 copy-start.17
  38.7 1.0 copy-start.2
  41.0 2.2 copy-start.3
  41.0 2.2 copy-start.18
  47.9 28.0 %all-to-all-start = ((bf16[2,2,128,288]{3,1,0,2:T(2,128)(2,1)}), bf16[2,2,128,288]{3,1,0,2:T(2,128)(2,1)S(1)}, u32[]{:S(2)}, u32[]{:S(2)}) async-start(bf16[2,2,128,288]{3,1,0,2:T(2,128)(2,1)} %copy.81), calls=%async_computation | async-start | bytes 786432 | tf_op jit(solution)/shard_map/all_to_all | solution.py:82
  52.5 98.8 %all-gather.11.cloned.1.call-start = ((), (), s32[]{:S(2)}) async-start(), calls=%async_computation.4 | async-start | bytes 1474560 | tf_op jit(solution)/shard_map/all_gather | solution.py:95
  55.4 152.9 %all-reduce.4.cloned.1.call-start = ((), (), s32[]{:S(2)}) async-start(), calls=%async_computation.7 | async-start | bytes 4718592 | tf_op jit(solution)/shard_map/psum | solution.py:102
  76.0 0.8 copy-start.9
  102.2 0.7 copy-start.19
  102.2 0.7 copy-start.20
  102.2 0.9 copy-start.12
  102.2 16.0 %copy-start.13 = (bf16[2048,16]{0,1:T(8,128)(2,1)S(1)}, bf16[2048,16]{0,1:T(8,128)(2,1)}, u32[]{:S(2)}) copy-start(bf16[2048,16]{0,1:T(8,128)(2,1)} %param.24) | copy-start | bytes 196612
  102.2 164.6 %reduce-scatter.2.cloned.1.call-start = ((), (), s32[]{:S(2)}) async-start(), calls=%async_computation.5 | async-start | bytes 2654208 | tf_op jit(solution)/shard_map/reduce_scatter | solution.py:126
  208.2 8.0 %copy-start.5 = (f32[2,128,1152]{1,0,2:T(2,128)S(1)}, f32[2,128,1152]{1,0,2:T(2,128)}, u32[]{:S(2)}) copy-start(f32[2,128,1152]{1,0,2:T(2,128)} %get-tuple-element.13) | copy-start | bytes 3538948
  208.2 8.0 %copy-start.7 = (f32[2,128,1152]{1,0,2:T(2,128)S(1)}, f32[2,128,1152]{1,0,2:T(2,128)}, u32[]{:S(2)}) copy-start(f32[2,128,1152]{1,0,2:T(2,128)} %reshape.78) | copy-start | bytes 3538948
  216.1 6.1 %copy-start.1 = (f32[2,128,1152]{1,0,2:T(2,128)}, f32[2,128,1152]{1,0,2:T(2,128)S(1)}, u32[]{:S(2)}) copy-start(f32[2,128,1152]{1,0,2:T(2,128)S(1)} %get-tuple-element.17) | copy-start | bytes 3538948
  216.1 1.5 copy-start.4
  216.1 1.5 copy-start.16
  222.2 1.2 copy-start.11
  225.3 0.7 copy-start.21
  225.3 41.5 %copy-start.10 = (bf16[288,256]{1,0:T(8,128)(2,1)S(1)}, bf16[288,256]{1,0:T(8,128)(2,1)}, u32[]{:S(2)}) copy-start(bf16[288,256]{1,0:T(8,128)(2,1)} %param.17) | copy-start | bytes 442372
  225.4 113.7 %all-gather.13.cloned.1.call-start = ((), (), s32[]{:S(2)}) async-start(), calls=%async_computation.6 | async-start | bytes 5308416 | tf_op jit(solution)/shard_map/all_gather | solution.py:139
  301.9 1.3 copy-start.8
  332.1 53.8 %copy-start.14 = (s32[1152]{0:T(1024)S(1)}, s32[1152]{0:T(1024)}, u32[]{:S(2)}) copy-start(s32[1152]{0:T(1024)} %param.32) | copy-start | bytes 13828
  385.9 44.1 %copy-start.15 = (f32[1152]{0:T(1024)S(1)}, f32[1152]{0:T(1024)}, u32[]{:S(2)}) copy-start(f32[1152]{0:T(1024)} %param.33) | copy-start | bytes 13828
Sparse Core Ops, SparseCore 0:
  9.9 26.7 all-gather.6
  41.1 38.9 all-gather.8
  81.7 29.1 all-gather.10
  113.2 94.9 all-reduce.3
  225.5 41.3 reduce-scatter.1
  298.4 40.5 all-gather.12
where the time goes:
time: 439 us; the launch traced here: 437 us
  waiting for transfers between devices  151 us (34%)
  blocking collectives  148 us (34%)
  other arithmetic  70.4 us (16%)
  local copies, waits for them, and re-layouts  29.1 us (7%)
  matrix products  19.6 us (4%)
  between operations  14.5 us (3%)
  starting transfers between devices  4.8 us (1%)
    psum x1, waiting for transfers between devices, per_device(): lax.psum((jnp.einsum('khvb,hkb->hvb', tiles, key, precision=highest), jnp...  54.1 us
    psum x1, blocking collectives, per_device(): lax.psum((local_total * shrink, local_weighted * shrink, local_pick), ('r...  41.3 us
    reduce_scatter x1, waiting for transfers between devices, per_device(): lax.psum_scatter(lax.dot_general(w_out, mine, (((0,), (0,)), ((), ())), p...  40.9 us
    pmax x1, blocking collectives, per_device(): top = lax.pmax(local_top, ('row', 'col'))  39.3 us
    add x1, other arithmetic, per_device(): alpha[None, :, None, :] * tiles + key_major[:, :, None, :] * write[None]  28.9 us
    all_gather x1, waiting for transfers between devices, per_device(): whole_rows = lax.all_gather(hidden_in, 'row', axis=1, tiled=True)  28 us
    all_to_all x1, waiting for transfers between devices, per_device(): lax.all_to_all(unit_pair, 'col', split_axis=2, concat_axis=3, tiled=True)  20.5 us
    unnamed x4, other arithmetic  17.7 us
  transfers between devices with their start and end apart: 7, of which 5 were waited for; matrix products, arithmetic and copies ran while one was open for 19% of the time, Pallas kernels for 0%

commit v1 on v0

--- a/solution.py
+++ b/solution.py
@@ -58,7 +58,14 @@
     key_rows = state.shape[0]
     batch = state.shape[2]
     vocab_dev = lm_weight.shape[1]
-    whole_rows = lax.all_gather(hidden_in, "row", axis=1, tiled=True)
+    size = lax.axis_size("row")
+    route_2 = [(i, (i + 1) % size) for i in range(size)]
+    parts = [hidden_in]
+    for hop in range(1, size):
+        parts = [lax.ppermute(parts[0], "row", route_2), *parts]
+    whole = jnp.concatenate(parts, axis=1)
+    shift = (lax.axis_index("row") + 1) * parts[-1].shape[1]
+    whole_rows = jnp.roll(whole, shift, axis=1)
     xfull = whole_rows.astype(jnp.float32)
     normed = (
         xfull

time: 439 us -> 449 us (1.023)
  waiting for transfers between devices: 151 us -> 161 us
    ppermute x0 -> x7, waiting for transfers between devices: none -> 38.4 us  [per_device(): parts = [lax.ppermute(parts[0], 'row', route_2), *parts]]
    all_gather x1 -> x0, waiting for transfers between devices: 28 us -> none  [per_device(): whole_rows = lax.all_gather(hidden_in, 'row', axis=1, tiled=True)]
    unnamed x51 -> x64, local copies, waits for them, and re-layouts: 8.76 us -> 9.04 us
  transfers between devices with their start and end apart: 7 -> 13, of which waited for: 5 -> 11; matrix products, arithmetic and copies ran while one was open for 19% -> 18% of each run, Pallas kernels for 0% -> 0%
where the time goes in v1:
time: 449 us; the launch traced here: 448 us
  waiting for transfers between devices  161 us (36%)
  blocking collectives  149 us (33%)
  other arithmetic  69.1 us (15%)
  local copies, waits for them, and re-layouts  29.4 us (7%)
  matrix products  19.5 us (4%)
  between operations  14.3 us (3%)
  starting transfers between devices  6.53 us (1%)
    psum x1, waiting for transfers between devices, per_device(): lax.psum((jnp.einsum('khvb,hkb->hvb', tiles, key, precision=highest), jnp...  55.5 us
    psum x1, blocking collectives, per_device(): lax.psum((local_total * shrink, local_weighted * shrink, local_pick), ('r...  41.3 us
    reduce_scatter x1, waiting for transfers between devices, per_device(): lax.psum_scatter(lax.dot_general(w_out, mine, (((0,), (0,)), ((), ())), p...  40.9 us
    pmax x1, blocking collectives, per_device(): top = lax.pmax(local_top, ('row', 'col'))  39.3 us
    ppermute x7, waiting for transfers between devices, per_device(): parts = [lax.ppermute(parts[0], 'row', route_2), *parts]  38.4 us
    add x1, other arithmetic, per_device(): alpha[None, :, None, :] * tiles + key_major[:, :, None, :] * write[None]  29 us
    unnamed x4, other arithmetic  17.7 us
    all_to_all x1, waiting for transfers between devices, per_device(): lax.all_to_all(unit_pair, 'col', split_axis=2, concat_axis=3, tiled=True)  17.7 us
  transfers between devices with their start and end apart: 13, of which 11 were waited for; matrix products, arithmetic and copies ran while one was open for 18% of the time, Pallas kernels for 0%

profile of v1, /device:TPU:0, one launch (start us, length us, event | category | flops | bytes accessed | tf_op | source)
XLA Modules:
  0.0 448.1 jit_solution(13755271509752090441)
XLA Ops:
  7.8 5.9 %collective-permute-done = bf16[288,256]{1,0:T(8,128)(2,1)S(1)} collective-permute-done((bf16[288,256]{1,0:T(8,128)(2,1)}, bf16[288,256]{1,0:T(8,128)(2,1)S(1)}, u32[]{:S(2)}, u32[]{:S(2)}) %collective-permute-start) | collective-permute-done | bytes 147488 | tf_op jit(solution)/shard_map/ppermute | solution.py:65
  13.7 5.5 %collective-permute-done.1 = bf16[288,256]{1,0:T(8,128)(2,1)S(1)} collective-permute-done((bf16[288,256]{1,0:T(8,128)(2,1)S(1)}, bf16[288,256]{1,0:T(8,128)(2,1)S(1)}, u32[]{:S(2)}, u32[]{:S(2)}) %collective-permute-start.1) | collective-permute-done | bytes 147488 | tf_op jit(solution)/shard_map/ppermute | solution.py:65
  19.2 5.5 %collective-permute-done.2 = bf16[288,256]{1,0:T(8,128)(2,1)S(1)} collective-permute-done((bf16[288,256]{1,0:T(8,128)(2,1)S(1)}, bf16[288,256]{1,0:T(8,128)(2,1)S(1)}, u32[]{:S(2)}, u32[]{:S(2)}) %collective-permute-start.2) | collective-permute-done | bytes 147488 | tf_op jit(solution)/shard_map/ppermute | solution.py:65
  24.6 5.5 %collective-permute-done.3 = bf16[288,256]{1,0:T(8,128)(2,1)S(1)} collective-permute-done((bf16[288,256]{1,0:T(8,128)(2,1)S(1)}, bf16[288,256]{1,0:T(8,128)(2,1)S(1)}, u32[]{:S(2)}, u32[]{:S(2)}) %collective-permute-start.3) | collective-permute-done | bytes 147488 | tf_op jit(solution)/shard_map/ppermute | solution.py:65
  30.1 5.5 %collective-permute-done.4 = bf16[288,256]{1,0:T(8,128)(2,1)S(1)} collective-permute-done((bf16[288,256]{1,0:T(8,128)(2,1)S(1)}, bf16[288,256]{1,0:T(8,128)(2,1)S(1)}, u32[]{:S(2)}, u32[]{:S(2)}) %collective-permute-start.4) | collective-permute-done | bytes 147488 | tf_op jit(solution)/shard_map/ppermute | solution.py:65
  35.6 5.6 %collective-permute-done.5 = bf16[288,256]{1,0:T(8,128)(2,1)} collective-permute-done((bf16[288,256]{1,0:T(8,128)(2,1)S(1)}, bf16[288,256]{1,0:T(8,128)(2,1)}, u32[]{:S(2)}, u32[]{:S(2)}) %collective-permute-start.5) | collective-permute-done | bytes 147488 | tf_op jit(solution)/shard_map/ppermute | solution.py:65
  41.8 5.1 %collective-permute-done.6 = bf16[288,256]{1,0:T(8,128)(2,1)} collective-permute-done((bf16[288,256]{1,0:T(8,128)(2,1)}, bf16[288,256]{1,0:T(8,128)(2,1)}, u32[]{:S(2)}, u32[]{:S(2)}) %collective-permute-start.6) | collective-permute-done | bytes 147488 | tf_op jit(solution)/shard_map/ppermute | solution.py:65
  47.8 0.9 constant_dynamic-update-slice_fusion.14
  48.9 0.9 constant_dynamic-update-slice_fusion.8
  49.8 0.9 constant_dynamic-update-slice_fusion.7
  52.5 1.0 copy-done.1
  53.5 1.2 convolution_bitcast_fusion.2
  54.8 2.2 fusion.8
  57.8 1.4 multiply_reduce_fusion.4
  59.2 1.1 copy.79
  60.6 1.1 copy.81
  61.7 5.6 %all-to-all-start = ((bf16[2,2,128,288]{3,1,0,2:T(2,128)(2,1)}), bf16[2,2,128,288]{3,1,0,2:T(2,128)(2,1)S(1)}, u32[]{:S(2)}, u32[]{:S(2)}) async-start(bf16[2,2,128,288]{3,1,0,2:T(2,128)(2,1)} %copy.81), calls=%async_computation | async-start | bytes 786432 | tf_op jit(solution)/shard_map/all_to_all | solution.py:89
  67.3 2.8 convolution_bitcast_fusion.1
  70.1 17.7 %all-to-all-done = bf16[2,2,128,288]{3,1,0,2:T(2,128)(2,1)S(1)} async-done(((bf16[2,2,128,288]{3,1,0,2:T(2,128)(2,1)}), bf16[2,2,128,288]{3,1,0,2:T(2,128)(2,1)S(1)}, u32[]{:S(2)}, u32[]{:S(2)}) %all-to-all-start) | async-done | bytes 294944 | tf_op jit(solution)/shard_map/all_to_all | solution.py:89
  89.8 17.5 %multiply_reduce_fusion = (f32[2,1152,128]{1,2,0:T(8,128)}, f32[2,1152,128]{1,2,0:T(8,128)}) fusion(f32[2,1152,32,128]{1,3,0,2:T(8,128)} %bitcast.104, f32[2,1152,32]{1,0,2:T(2,128)S(1)} %copy.112, f32[2,1152,32]{1,0,2:T(2,128)S(1)} %copy.111), kind=kLoop, calls=%fused_computation.2 | loop fusion | flops 37158912 | bytes 40697856
  107.3 3.4 copy.107
  110.7 3.4 copy.99
  114.3 1.7 fusion.28
  116.1 13.3 %all-gather.1 = f32[4,288,2]{1,2,0:T(2,128)S(1)} all-gather(f32[1,288,2]{1,2,0:T(2,128)S(1)} %divide_bitcast_fusion), channel_id=1, replica_groups=mesh['row'=8,'col'=4] {'col'}, dimensions={0}, use_global_device_ids=true | all-gather | bytes 11520 | tf_op jit(solution)/shard_map/all_gather | solution.py:104
  129.5 1.7 fusion.27
  131.3 13.8 %all-gather = f32[4,288,2]{1,2,0:T(2,128)S(1)} all-gather(f32[1,288,2]{1,2,0:T(2,128)S(1)} %fusion.18), channel_id=1, replica_groups=mesh['row'=8,'col'=4] {'col'}, dimensions={0}, use_global_device_ids=true | all-gather | bytes 11520 | tf_op jit(solution)/shard_map/all_gather | solution.py:103
  145.2 1.1 copy.86
  146.5 1.1 multiply_reduce_fusion.5
  147.7 12.0 %psum.51 = f32[2,1152]{1,0:T(2,128)S(1)} all-reduce(f32[2,1152]{1,0:T(2,128)S(1)} %reduce_sum.77), channel_id=1, replica_groups=mesh['row'=8,'col'=4] {'col'}, use_global_device_ids=true, to_apply=%region_5.6 | all-reduce | flops 2304 | bytes 18432 | tf_op jit(solution)/shard_map/psum | solution.py:109
  159.7 1.1 copy.89
  160.8 2.8 reshape.76
  163.5 2.8 reshape.78
  166.3 55.5 %all-reduce.4.cloned.1.call-done = (f32[2,128,1152]{1,0,2:T(2,128)}, f32[2,128,1152]{1,0,2:T(2,128)}) async-done(((f32[2,128,1152]{1,0,2:T(2,128)}, f32[2,128,1152]{1,0,2:T(2,128)}), (f32[2,128,1152]{1,0,2:T(2,128)}, f32[2,128,1152]{1,0,2:T(2,128)})) %all-reduce.4.cloned.1.call-update) | async-done | bytes 2359312 | tf_op jit(solution)/shard_map/psum | solution.py:109
  221.8 7.9 %multiply_reduce_fusion.3 = (f32[2,1152]{0,1:T(8,128)S(1)}, f32[2,128,1152]{1,0,2:T(2,128)S(1)}) fusion(f32[2,1152]{0,1:T(8,128)} %copy.89, f32[2,128,1152]{1,0,2:T(2,128)} %get-tuple-element.13, f32[2,1152]{0,1:T(8,128)S(1)} %copy.77, f32[2,128,1152]{1,0,2:T(2,128)} %reshape.76, f32[2,128,1152]{1,0,2:T(2,128)} %get-tuple-element.12, f32[2,1152]{0,1:T(8,128)} %copy.86), kind=kLoop, calls=%fused_computation.16 | loop fusion | flops 2356992 | bytes 4755456 | tf_op jit(solution)/shard_map/reduce_sum | solution.py:120
  229.9 4.6 %fusion.6 = bf16[2,128,1152]{1,0,2:T(2,128)(2,1)S(1)} fusion(f32[2,128,1152]{1,0,2:T(2,128)S(1)} %copy-done.6, f32[128]{0:T(128)S(1)} %copy-done.15, f32[2,1152]{0,1:T(8,128)S(1)} %add_rsqrt_fusion, f32[2,128,1152]{1,0,2:T(2,128)S(1)} %get-tuple-element.17, f32[2,1152]{0,1:T(8,128)S(1)} %copy-done.4, f32[2,128,1152]{1,0,2:T(2,128)S(1)} %copy-done.5, ...), kind=kLoop, calls=%fused_computation.19 | loop fusion | flops 3244032 | bytes 4156928 | tf_op jit(solution)/shard_map/convert_element_type | solution.py:131
  234.6 1.9 convolution_bitcast_fusion
  237.2 40.9 %reduce-scatter.2.cloned.1.call-done = f32[256,288]{0,1:T(8,128)} async-done(((f32[2048,288]{0,1:T(8,128)}), f32[256,288]{0,1:T(8,128)}) %reduce-scatter.2.cloned.1.call-update) | async-done | bytes 294928 | tf_op jit(solution)/shard_map/reduce_scatter | solution.py:133
  278.0 1.1 multiply_reduce_fusion.6
  279.1 12.5 %psum.52 = f32[288]{0:T(512)S(1)} all-reduce(f32[288]{0:T(512)S(1)} %multiply_reduce_fusion.6), channel_id=1, replica_groups=mesh['row'=8,'col'=4] {'row'}, use_global_device_ids=true, to_apply=%region_9.10 | all-reduce | flops 288 | bytes 2304 | tf_op jit(solution)/shard_map/psum | solution.py:140
  291.7 1.1 multiply_convert_fusion
  292.7 16.5 %all_gather.22 = bf16[1152,256]{1,0:T(8,128)(2,1)} all-gather(bf16[288,256]{1,0:T(8,128)(2,1)S(1)} %multiply_convert_fusion), channel_id=1, replica_groups=mesh['row'=8,'col'=4] {'col'}, dimensions={0}, use_global_device_ids=true | all-gather | bytes 737280 | tf_op jit(solution)/shard_map/all_gather | solution.py:144
  309.5 3.4 copy.109
  313.0 29.0 %fusion = f32[32,256,1152]{2,1,0:T(8,128)} fusion(f32[32,256,1152]{2,1,0:T(8,128)} %param.18, f32[256,1152]{1,0:T(8,128)} %bitcast.107, f32[32,2,1152]{2,1,0:T(2,128)S(1)} %copy.84, f32[256,1152]{1,0:T(8,128)S(1)} %bitcast.108), kind=kLoop, calls=%fused_computation.1 | loop fusion | flops 28311552 | bytes 78151680 | tf_op jit(solution)/shard_map/add | solution.py:118
  342.1 7.9 %all-gather.10.cloned.1.call-done = bf16[1152,2048]{1,0:T(8,128)(2,1)} async-done(((bf16[1152,256]{1,0:T(8,128)(2,1)}), bf16[1152,2048]{1,0:T(8,128)(2,1)}) %all-gather.10.cloned.1.call-update) | async-done | bytes 4718608 | tf_op jit(solution)/shard_map/all_gather | solution.py:146
  350.0 7.6 %fusion.26 = (f32[1152]{0:T(1024)S(1)}, f32[1152,640]{0,1:T(8,128)}) fusion(bf16[1152,2048]{1,0:T(8,128)(2,1)} %all-gather.10.cloned.1.call-done, bf16[2048,640]{1,0:T(8,128)(2,1)S(1)} %copy-done), kind=kOutput, calls=%fused_computation.84 | convolution fusion | flops 3020635136 | bytes 10293760 | tf_op jit(solution)/shard_map/dot_general | solution.py:145
  357.6 39.3 %pmax.7 = f32[1152]{0:T(1024)S(1)} all-reduce(f32[1152]{0:T(1024)S(1)} %get-tuple-element.25), channel_id=1, replica_groups=mesh['row'=8,'col'=4] {'row','col'}, use_global_device_ids=true, to_apply=%region_13.14 | all-reduce | flops 1152 | bytes 9216 | tf_op jit(solution)/shard_map/pmax | solution.py:157
  396.9 2.7 multiply_reduce_fusion.2
  399.6 41.3 %all-reduce = (f32[1152]{0:T(1024)S(1)}, f32[1152]{0:T(1024)S(1)}, f32[1152]{0:T(1024)S(1)}) all-reduce(f32[1152]{0:T(1024)S(1)} %get-tuple-element.8, f32[1152]{0:T(1024)S(1)} %get-tuple-element.24, f32[1152]{0:T(1024)S(1)} %get-tuple-element.23), channel_id=1, replica_groups=mesh['row'=8,'col'=4] {'row','col'}, use_global_device_ids=true, to_apply=%region_11.12 | all-reduce | flops 3456 | bytes 27648 | tf_op jit(solution)/shard_map/psum | solution.py:159
  (111 shorter events, 9.7 us)
Async XLA Ops:
  7.2 342.8 %copy-start = (bf16[2048,640]{1,0:T(8,128)(2,1)S(1)}, bf16[2048,640]{1,0:T(8,128)(2,1)}, u32[]{:S(2)}) copy-start(bf16[2048,640]{1,0:T(8,128)(2,1)} %param.31) | copy-start | bytes 7864324
  7.2 44.6 %copy-start.8 = (bf16[288,256]{1,0:T(8,128)(2,1)S(1)}, bf16[288,256]{1,0:T(8,128)(2,1)}, u32[]{:S(2)}) copy-start(bf16[288,256]{1,0:T(8,128)(2,1)} %param.17) | copy-start | bytes 442372
  7.2 153.6 %all-gather.6.cloned.1.call-start = ((), (), s32[]{:S(2)}) async-start(), calls=%async_computation.2 | async-start | bytes 1474560 | tf_op jit(solution)/shard_map/all_gather | solution.py:101
  7.2 6.5 %collective-permute-start = (bf16[288,256]{1,0:T(8,128)(2,1)}, bf16[288,256]{1,0:T(8,128)(2,1)S(1)}, u32[]{:S(2)}, u32[]{:S(2)}) collective-permute-start(bf16[288,256]{1,0:T(8,128)(2,1)} %param.17), channel_id=1, source_target_pairs={{0,4},{4,8},{8,12},{12,16},{16,20},{20,24},{24,28},{28,0},{1,5},{5... | collective-permute-start | bytes 442376 | tf_op jit(solution)/shard_map/ppermute | solution.py:65
  13.7 5.5 %collective-permute-start.1 = (bf16[288,256]{1,0:T(8,128)(2,1)S(1)}, bf16[288,256]{1,0:T(8,128)(2,1)S(1)}, u32[]{:S(2)}, u32[]{:S(2)}) collective-permute-start(bf16[288,256]{1,0:T(8,128)(2,1)S(1)} %collective-permute-done), channel_id=1, source_target_pairs={{0,4},{4,8},{8,12},{12,16},{16,20},{20,24},{24,28},{28,0},{1,5},{5... | collective-permute-start | bytes 442376 | tf_op jit(solution)/shard_map/ppermute | solution.py:65
  19.2 5.5 %collective-permute-start.2 = (bf16[288,256]{1,0:T(8,128)(2,1)S(1)}, bf16[288,256]{1,0:T(8,128)(2,1)S(1)}, u32[]{:S(2)}, u32[]{:S(2)}) collective-permute-start(bf16[288,256]{1,0:T(8,128)(2,1)S(1)} %collective-permute-done.1), channel_id=1, source_target_pairs={{0,4},{4,8},{8,12},{12,16},{16,20},{20,24},{24,28},{28,0},{1,5},{5... | collective-permute-start | bytes 442376 | tf_op jit(solution)/shard_map/ppermute | solution.py:65
  24.6 5.5 %collective-permute-start.3 = (bf16[288,256]{1,0:T(8,128)(2,1)S(1)}, bf16[288,256]{1,0:T(8,128)(2,1)S(1)}, u32[]{:S(2)}, u32[]{:S(2)}) collective-permute-start(bf16[288,256]{1,0:T(8,128)(2,1)S(1)} %collective-permute-done.2), channel_id=1, source_target_pairs={{0,4},{4,8},{8,12},{12,16},{16,20},{20,24},{24,28},{28,0},{1,5},{5... | collective-permute-start | bytes 442376 | tf_op jit(solution)/shard_map/ppermute | solution.py:65
  30.1 5.5 %collective-permute-start.4 = (bf16[288,256]{1,0:T(8,128)(2,1)S(1)}, bf16[288,256]{1,0:T(8,128)(2,1)S(1)}, u32[]{:S(2)}, u32[]{:S(2)}) collective-permute-start(bf16[288,256]{1,0:T(8,128)(2,1)S(1)} %collective-permute-done.3), channel_id=1, source_target_pairs={{0,4},{4,8},{8,12},{12,16},{16,20},{20,24},{24,28},{28,0},{1,5},{5... | collective-permute-start | bytes 442376 | tf_op jit(solution)/shard_map/ppermute | solution.py:65
  35.6 5.6 %collective-permute-start.5 = (bf16[288,256]{1,0:T(8,128)(2,1)S(1)}, bf16[288,256]{1,0:T(8,128)(2,1)}, u32[]{:S(2)}, u32[]{:S(2)}) collective-permute-start(bf16[288,256]{1,0:T(8,128)(2,1)S(1)} %collective-permute-done.4), channel_id=1, source_target_pairs={{0,4},{4,8},{8,12},{12,16},{16,20},{20,24},{24,28},{28,0},{1,5},{5... | collective-permute-start | bytes 442376 | tf_op jit(solution)/shard_map/ppermute | solution.py:65
  41.1 5.8 %collective-permute-start.6 = (bf16[288,256]{1,0:T(8,128)(2,1)}, bf16[288,256]{1,0:T(8,128)(2,1)}, u32[]{:S(2)}, u32[]{:S(2)}) collective-permute-start(bf16[288,256]{1,0:T(8,128)(2,1)} %collective-permute-done.5), channel_id=1, source_target_pairs={{0,4},{4,8},{8,12},{12,16},{16,20},{20,24},{24,28},{28,0},{1,5},{5... | collective-permute-start | bytes 442376 | tf_op jit(solution)/shard_map/ppermute | solution.py:65
  51.7 1.8 copy-start.16
  52.5 1.0 copy-start.1
  54.8 2.2 copy-start.2
  54.8 2.2 copy-start.17
  61.7 26.2 %all-to-all-start = ((bf16[2,2,128,288]{3,1,0,2:T(2,128)(2,1)}), bf16[2,2,128,288]{3,1,0,2:T(2,128)(2,1)S(1)}, u32[]{:S(2)}, u32[]{:S(2)}) async-start(bf16[2,2,128,288]{3,1,0,2:T(2,128)(2,1)} %copy.81), calls=%async_computation | async-start | bytes 786432 | tf_op jit(solution)/shard_map/all_to_all | solution.py:89
  67.3 96.2 %all-gather.8.cloned.1.call-start = ((), (), s32[]{:S(2)}) async-start(), calls=%async_computation.3 | async-start | bytes 1474560 | tf_op jit(solution)/shard_map/all_gather | solution.py:102
  70.1 151.7 %all-reduce.4.cloned.1.call-start = ((), (), s32[]{:S(2)}) async-start(), calls=%async_computation.6 | async-start | bytes 4718592 | tf_op jit(solution)/shard_map/psum | solution.py:109
  87.9 0.7 copy-start.7
  110.7 3.5 copy-start.18
  110.7 3.6 copy-start.19
  110.7 3.6 copy-start.11
  114.1 15.4 %copy-start.12 = (bf16[2048,16]{0,1:T(8,128)(2,1)S(1)}, bf16[2048,16]{0,1:T(8,128)(2,1)}, u32[]{:S(2)}) copy-start(bf16[2048,16]{0,1:T(8,128)(2,1)} %param.24) | copy-start | bytes 196612
  114.1 163.9 %reduce-scatter.2.cloned.1.call-start = ((), (), s32[]{:S(2)}) async-start(), calls=%async_computation.4 | async-start | bytes 2654208 | tf_op jit(solution)/shard_map/reduce_scatter | solution.py:133
  221.8 8.0 %copy-start.4 = (f32[2,1152]{0,1:T(8,128)S(1)}, f32[2,1152]{0,1:T(8,128)}, u32[]{:S(2)}) copy-start(f32[2,1152]{0,1:T(8,128)} %copy.89) | copy-start | bytes 27652
  221.8 8.0 %copy-start.5 = (f32[2,128,1152]{1,0,2:T(2,128)S(1)}, f32[2,128,1152]{1,0,2:T(2,128)}, u32[]{:S(2)}) copy-start(f32[2,128,1152]{1,0,2:T(2,128)} %get-tuple-element.13) | copy-start | bytes 3538948
  221.8 8.0 %copy-start.6 = (f32[2,128,1152]{1,0,2:T(2,128)S(1)}, f32[2,128,1152]{1,0,2:T(2,128)}, u32[]{:S(2)}) copy-start(f32[2,128,1152]{1,0,2:T(2,128)} %reshape.78) | copy-start | bytes 3538948
  221.8 8.0 %copy-start.15 = (f32[128]{0:T(128)S(1)}, f32[128]{0:T(128)}, u32[]{:S(2)}) copy-start(f32[128]{0:T(128)} %param.28) | copy-start | bytes 1540
  229.7 4.8 %copy-start.3 = (f32[2,128,1152]{1,0,2:T(2,128)}, f32[2,128,1152]{1,0,2:T(2,128)S(1)}, u32[]{:S(2)}) copy-start(f32[2,128,1152]{1,0,2:T(2,128)S(1)} %get-tuple-element.17) | copy-start | bytes 3538948
  229.9 4.7 %copy-start.10 = (bf16[256,2048]{1,0:T(8,128)(2,1)S(1)}, bf16[256,2048]{1,0:T(8,128)(2,1)}, u32[]{:S(2)}) copy-start(bf16[256,2048]{1,0:T(8,128)(2,1)} %param.29) | copy-start | bytes 3145732
  236.5 0.7 copy-start.20
  236.5 41.5 %copy-start.9 = (bf16[288,256]{1,0:T(8,128)(2,1)S(1)}, bf16[288,256]{1,0:T(8,128)(2,1)}, u32[]{:S(2)}) copy-start(bf16[288,256]{1,0:T(8,128)(2,1)} %param.17) | copy-start | bytes 442372
  236.5 113.5 %all-gather.10.cloned.1.call-start = ((), (), s32[]{:S(2)}) async-start(), calls=%async_computation.5 | async-start | bytes 5308416 | tf_op jit(solution)/shard_map/all_gather | solution.py:146
  342.1 54.8 %copy-start.13 = (s32[1152]{0:T(1024)S(1)}, s32[1152]{0:T(1024)}, u32[]{:S(2)}) copy-start(s32[1152]{0:T(1024)} %param.32) | copy-start | bytes 13828
  357.6 83.3 %copy-start.14 = (f32[1152]{0:T(1024)S(1)}, f32[1152]{0:T(1024)}, u32[]{:S(2)}) copy-start(f32[1152]{0:T(1024)} %param.33) | copy-start | bytes 13828
Sparse Core Ops, SparseCore 0:
  54.9 39.4 all-gather.5
  95.9 28.5 all-gather.7
  127.0 94.8 all-reduce.3
  236.6 41.3 reduce-scatter.1
  309.4 40.5 all-gather.9
